TPU v7x, 128 devices: a whole 4x4x4 slice. The times are simulated.
128 devices in a mesh: row: 8 (over z_lo, y), col: 16 (over z_hi, x, core).
Axes of the slice: x: 4, y: 4, z: 4 (z_hi: 2, z_lo: 2; z = z_hi * 2 + z_lo), core: 2. Of those that a mesh axis runs over, the one named last changes fastest.
Arguments:
- observed: float32 [4, 65536], P(None, ('row', 'col')), may hold values from -50 to 50
- tile_values: bfloat16 [256, 32, 256, 256], P('row', 'col'), may hold values from -2.2649514 to 2.2649514
- tile_cols: int32 [256, 32], P('row', 'col'), may hold values from 0 to 255
Outputs:
- solution: float32 [4, 1048576], P(None, ('col', 'row'))
- residual_ratio: float32 [4], replicated
All inputs are finite; a program needn't handle non-finite values.
Results may differ from a plain program's by a relative error of at most 0.0021.
Values may be sent and summed in bfloat16 or wider, within the bound.
A program may use at most 128 MiB of HBM per device.

v0:
```python
import jax
import jax.numpy as jnp
from jax import lax
from jax.sharding import PartitionSpec as P

ITERS = 2
N = 1048576
epsilon_sq = 1e-06


def local(observed, tile_values, tile_cols):
    right_sides = observed.shape[0]
    row_tiles = tile_values.shape[0]
    per_block = tile_values.shape[1]
    tile_size = tile_values.shape[2]
    col_tiles = N // (tile_size * lax.axis_size("col"))
    panel_len = col_tiles * tile_size
    share_len = panel_len // lax.axis_size("row")
    flat_cols = tile_cols.reshape(-1)

    def adjoint_map(left_bf):
        gathered = lax.all_gather(left_bf, "col", axis=1, tiled=True).reshape(
            right_sides, row_tiles, tile_size
        )
        tile_terms = jnp.einsum(
            "rktj,nrt->nrkj", tile_values, gathered, preferred_element_type=jnp.float32
        )
        tile_terms = tile_terms.reshape(right_sides, row_tiles * per_block, tile_size)
        placed = (
            jnp.zeros((right_sides, col_tiles, tile_size), jnp.float32)
            .at[:, flat_cols]
            .add(tile_terms)
        )
        placed = placed.reshape(right_sides, panel_len)
        summed = lax.psum_scatter(placed, "row", scatter_dimension=1, tiled=True)
        return summed

    def lanczos_pair(left_raw, right_vec):
        beta_sq = lax.psum(jnp.sum(left_raw * left_raw, axis=1), ("row", "col"))
        beta_norm = jnp.sqrt(beta_sq + epsilon_sq)
        product = adjoint_map(left_raw.astype(jnp.bfloat16))
        right_raw = product / beta_norm[:, None] - beta_norm[:, None] * right_vec
        alpha_sq = lax.psum(jnp.sum(right_raw * right_raw, axis=1), ("row", "col"))
        alpha_norm = jnp.sqrt(alpha_sq + epsilon_sq)
        return (beta_norm, alpha_norm, right_raw)

    blank_right = jnp.zeros((right_sides, share_len), jnp.float32)
    beta_norm, alpha_norm, right_raw = lanczos_pair(observed, blank_right)
    first_beta = beta_norm
    left_vec = observed / beta_norm[:, None]
    right_vec = right_raw / alpha_norm[:, None]
    right_bf = right_raw.astype(jnp.bfloat16)
    phibar = beta_norm
    rhobar = alpha_norm
    direction = right_vec
    solution = jnp.zeros_like(right_vec)
    for iteration in range(ITERS):
        whole_panel = lax.all_gather(right_bf, "row", axis=1, tiled=True)
        picked = jnp.take(whole_panel.reshape(right_sides, col_tiles, tile_size), tile_cols, axis=1)
        partial_rows = jnp.einsum(
            "rktj,nrkj->nrt", tile_values, picked, preferred_element_type=jnp.float32
        )
        left_raw = (
            lax.psum_scatter(
                partial_rows.reshape(right_sides, row_tiles * tile_size),
                "col",
                scatter_dimension=1,
                tiled=True,
            )
            / alpha_norm[:, None]
            - alpha_norm[:, None] * left_vec
        )
        beta_norm, alpha_norm, right_raw = lanczos_pair(left_raw, right_vec)
        left_vec = left_raw / beta_norm[:, None]
        right_vec = right_raw / alpha_norm[:, None]
        right_bf = right_raw.astype(jnp.bfloat16)
        rho_val = jnp.sqrt(rhobar * rhobar + beta_norm * beta_norm)
        cosine = rhobar / rho_val
        sine_val = beta_norm / rho_val
        theta_val = sine_val * alpha_norm
        rhobar = -cosine * alpha_norm
        phi_val = cosine * phibar
        phibar = sine_val * phibar
        solution = solution + (phi_val / rho_val)[:, None] * direction
        direction = right_vec - (theta_val / rho_val)[:, None] * direction
    return (solution, phibar / first_beta)


def solution(mesh):
    in_specs = (P(None, ("row", "col")), P("row", "col", None, None), P("row", "col"))
    out_specs = (P(None, ("col", "row")), P())
    return jax.shard_map(local, mesh=mesh, in_specs=in_specs, out_specs=out_specs, check_vma=False)
```

profile of v0, /device:TPU:1, one launch (start us, length us, event | category | flops | bytes accessed | tf_op | source)
XLA Modules:
  0.0 1160.2 jit_solution(9524676217768432283)
XLA Ops:
  7.2 0.0 reduce-scatter.13.cloned.1.call-start
  7.2 0.9 fusion.20
  8.1 26.5 %all_gather.12 = bf16[4,8192]{1,0:T(4,128)(2,1)S(1)} all-gather(bf16[4,512]{1,0:T(4,128)(2,1)S(1)} %get-tuple-element.13), channel_id=1, replica_groups=mesh['row'=8,'col'=16] {'col'}, dimensions={1}, use_global_device_ids=true | all-gather | bytes 69632 | tf_op jit(solution)/shard_map/all_gather | solution.py:22
  34.6 0.8 copy.17
  35.4 0.1 reshape.77
  35.5 4.6 fusion.21
  40.0 0.1 broadcast.38.clone
  40.2 2.8 scatter_fusion
  43.0 16.1 %copy.26 = f32[4,65536]{0,1:T(8,128)} copy(f32[4,65536]{1,0:T(4,128)S(1)} %bitcast.65) | data formatting | bytes 2097152
  59.1 0.0 copy-start.1
  59.1 0.0 reduce-scatter.13.cloned.1.call-update
  59.1 0.0 reduce-scatter.15.cloned.1.call-start
  59.2 369.9 %psum.35 = f32[4]{0:T(128)S(1)} all-reduce(f32[4]{0:T(128)S(1)} %get-tuple-element.14), channel_id=1, replica_groups=mesh['row'=8,'col'=16] {'row','col'}, use_global_device_ids=true, to_apply=%region_3.0 | all-reduce | flops 4 | bytes 32 | tf_op jit(solution)/shard_map/psum | solution.py:39
  429.1 0.0 copy-done.1
  429.1 0.1 copy.19
  429.2 0.1 reshape.124
  429.3 0.1 copy.18
  429.4 0.0 reduce-scatter.13.cloned.1.call-done
  429.5 2.8 copy.27
  432.3 0.3 multiply_reduce_fusion.1
  432.6 22.8 %all_gather.13 = bf16[4,65536]{1,0:T(4,128)(2,1)S(1)} all-gather(bf16[4,8192]{1,0:T(4,128)(2,1)S(1)} %convert_element_type.13), channel_id=1, replica_groups=mesh['row'=8,'col'=16] {'row'}, dimensions={1}, use_global_device_ids=true | all-gather | bytes 589824 | tf_op jit(solution)/shard_map/all_gather | solution.py:58
  455.4 0.7 gather_fusion
  456.1 0.0 copy-start
  456.1 5.7 fusion.2
  461.8 2.6 copy.28
  464.4 0.0 reduce-scatter.15.cloned.1.call-update
  464.5 0.0 reduce-scatter.17.cloned.1.call-start
  464.5 74.8 %psum.36 = f32[4]{0:T(128)S(1)} all-reduce(f32[4]{0:T(128)S(1)} %get-tuple-element.11), channel_id=1, replica_groups=mesh['row'=8,'col'=16] {'row','col'}, use_global_device_ids=true, to_apply=%region_5.0 | all-reduce | flops 4 | bytes 32 | tf_op jit(solution)/shard_map/psum | solution.py:43
  539.4 8.0 reduce-scatter.15.cloned.1.call-done
  547.4 1.1 copy.29
  548.4 0.0 copy-done
  548.4 0.2 multiply_reduce_fusion.2
  548.7 23.2 %all_gather.14 = bf16[4,8192]{1,0:T(4,128)(2,1)S(1)} all-gather(bf16[4,512]{1,0:T(4,128)(2,1)S(1)} %convert_element_type.14), channel_id=1, replica_groups=mesh['row'=8,'col'=16] {'col'}, dimensions={1}, use_global_device_ids=true | all-gather | bytes 69632 | tf_op jit(solution)/shard_map/all_gather | solution.py:22
  571.8 4.6 fusion.22
  576.4 0.1 broadcast.38
  576.6 2.8 scatter_fusion.1
  579.4 16.1 %copy.30 = f32[4,65536]{0,1:T(8,128)} copy(f32[4,65536]{1,0:T(4,128)S(1)} %bitcast.64) | data formatting | bytes 2097152
  595.5 0.0 reduce-scatter.17.cloned.1.call-update
  595.5 0.0 reduce-scatter.19.cloned.1.call-start
  595.6 371.7 %psum.37 = f32[4]{0:T(128)S(1)} all-reduce(f32[4]{0:T(128)S(1)} %get-tuple-element.9), channel_id=1, replica_groups=mesh['row'=8,'col'=16] {'row','col'}, use_global_device_ids=true, to_apply=%region_8.10 | all-reduce | flops 4 | bytes 32 | tf_op jit(solution)/shard_map/psum | solution.py:39
  967.3 0.0 reduce-scatter.17.cloned.1.call-done
  967.3 2.8 copy.31
  970.2 0.1 fusion.19
  970.3 23.0 %all_gather.15 = bf16[4,65536]{1,0:T(4,128)(2,1)S(1)} all-gather(bf16[4,8192]{1,0:T(4,128)(2,1)S(1)} %get-tuple-element.7), channel_id=1, replica_groups=mesh['row'=8,'col'=16] {'row'}, dimensions={1}, use_global_device_ids=true | all-gather | bytes 589824 | tf_op jit(solution)/shard_map/all_gather | solution.py:58
  993.3 0.7 gather_fusion.1
  994.0 5.7 fusion
  999.7 2.6 copy.32
  1002.3 0.2 multiply_reduce_fusion
  1002.5 0.0 reduce-scatter.19.cloned.1.call-update
  1002.5 75.0 %psum.38 = f32[4]{0:T(128)S(1)} all-reduce(f32[4]{0:T(128)S(1)} %multiply_reduce_fusion), channel_id=1, replica_groups=mesh['row'=8,'col'=16] {'row','col'}, use_global_device_ids=true, to_apply=%region_12.14 | all-reduce | flops 4 | bytes 32 | tf_op jit(solution)/shard_map/psum | solution.py:43
  1077.5 8.0 reduce-scatter.19.cloned.1.call-done
  1085.5 1.1 copy.33
  1086.5 0.2 fusion.11
  1086.7 65.6 %psum.39 = f32[4]{0:T(128)S(1)} all-reduce(f32[4]{0:T(128)S(1)} %fusion.11), channel_id=1, replica_groups=mesh['row'=8,'col'=16] {'row','col'}, use_global_device_ids=true, to_apply=%region_15.17 | all-reduce | flops 4 | bytes 32 | tf_op jit(solution)/shard_map/psum | solution.py:39
  1152.3 0.6 multiply_divide_fusion
  1152.9 0.8 multiply_add_fusion
  (11 shorter events, 0.1 us)
Async XLA Ops:
  7.2 422.3 %reduce-scatter.13.cloned.1.call-start = ((), (), s32[]{:S(2)}) async-start(), calls=%async_computation.4 | async-start | bytes 37748736
  59.1 370.0 %copy-start.1 = (s32[32,2]{0,1:T(2,128)S(1)}, s32[32,2]{0,1:T(2,128)}, u32[]{:S(2)}) copy-start(s32[32,2]{0,1:T(2,128)} %param.7) | copy-start | bytes 772
  59.1 488.2 %reduce-scatter.15.cloned.1.call-start = ((), (), s32[]{:S(2)}) async-start(), calls=%async_computation.5 | async-start | bytes 4456448
  456.1 92.3 %copy-start = (f32[4,512]{1,0:T(4,128)S(1)}, f32[4,512]{1,0:T(4,128)}, u32[]{:S(2)}) copy-start(f32[4,512]{1,0:T(4,128)} %param.5) | copy-start | bytes 24580
  464.5 502.9 %reduce-scatter.17.cloned.1.call-start = ((), (), s32[]{:S(2)}) async-start(), calls=%async_computation.6 | async-start | bytes 37748736
  595.5 490.0 %reduce-scatter.19.cloned.1.call-start = ((), (), s32[]{:S(2)}) async-start(), calls=%async_computation.7 | async-start | bytes 4456448
Sparse Core Ops, SparseCore 0:
  59.3 325.6 reduce-scatter.12
  464.6 82.7 reduce-scatter.14
  595.6 327.5 reduce-scatter.16
  1002.6 82.7 reduce-scatter.18
where the time goes:
time: 1160 us
  blocking collectives  1050 us (91%)
  local copies, waits for them, and re-layouts  48 us (4%)
  matrix products  20.5 us (2%)
  waiting for transfers between devices  16.1 us (1%)
  between operations  13.9 us (1%)
    psum x3, blocking collectives, lanczos_pair(): beta_sq = lax.psum(jnp.sum(left_raw * left_raw, axis=1), ('row', 'col'))  807 us
    psum x2, blocking collectives, lanczos_pair(): alpha_sq = lax.psum(jnp.sum(right_raw * right_raw, axis=1), ('row', 'col'))  150 us
    all_gather x2, blocking collectives, adjoint_map(): lax.all_gather(left_bf, 'col', axis=1, tiled=True)  49.7 us
    unnamed x13, local copies, waits for them, and re-layouts  46 us
    all_gather x2, blocking collectives, local(): whole_panel = lax.all_gather(right_bf, 'row', axis=1, tiled=True)  45.8 us
  transfers between devices with their start and end apart: 4, of which 2 were waited for; matrix products, arithmetic and copies ran while one was open for 0% of the time, Pallas kernels for 0%

commit v1 on v0

--- a/solution.py
+++ b/solution.py
@@ -40,7 +40,7 @@
         beta_norm = jnp.sqrt(beta_sq + epsilon_sq)
         product = adjoint_map(left_raw.astype(jnp.bfloat16))
         right_raw = product / beta_norm[:, None] - beta_norm[:, None] * right_vec
-        alpha_sq = lax.psum(jnp.sum(right_raw * right_raw, axis=1), ("row", "col"))
+        alpha_sq = lax.psum(lax.psum(jnp.sum(right_raw * right_raw, axis=1), "row"), "col")
         alpha_norm = jnp.sqrt(alpha_sq + epsilon_sq)
         return (beta_norm, alpha_norm, right_raw)
 

time: 1160 us -> 1190 us (1.026)
  waiting for transfers between devices: 16.1 us -> 85.8 us
  blocking collectives: 1050 us -> 1020 us
    unnamed x8, waiting for transfers between devices: 16.1 us -> 85.8 us
    psum x2 -> x4, blocking collectives: 150 us -> 113 us  [the longest x2 85.2 us: lanczos_pair(): lax.psum(lax.psum(jnp.sum(right_raw * right_raw, axis=1), 'row'), 'col')]
where the time goes in v1:
time: 1190 us
  blocking collectives  1020 us (86%)
  waiting for transfers between devices  85.8 us (7%)
  local copies, waits for them, and re-layouts  48 us (4%)
  matrix products  20.5 us (2%)
  between operations  13.9 us (1%)
    psum x3, blocking collectives, lanczos_pair(): beta_sq = lax.psum(jnp.sum(left_raw * left_raw, axis=1), ('row', 'col'))  808 us
    unnamed x8, waiting for transfers between devices  85.8 us
    psum x2, blocking collectives, lanczos_pair(): lax.psum(lax.psum(jnp.sum(right_raw * right_raw, axis=1), 'row'), 'col')  85.2 us
    all_gather x2, blocking collectives, adjoint_map(): lax.all_gather(left_bf, 'col', axis=1, tiled=True)  49.6 us
    unnamed x13, local copies, waits for them, and re-layouts  46 us
    all_gather x2, blocking collectives, local(): whole_panel = lax.all_gather(right_bf, 'row', axis=1, tiled=True)  45.8 us
    psum x2, blocking collectives, lanczos_pair(): lax.psum(jnp.sum(right_raw * right_raw, axis=1), 'row')  28.1 us
  transfers between devices with their start and end apart: 4, of which 2 were waited for; matrix products, arithmetic and copies ran while one was open for 0% of the time, Pallas kernels for 0%

profile of v1, /device:TPU:1, one launch (start us, length us, event | category | flops | bytes accessed | tf_op | source)
XLA Modules:
  0.0 1193.8 jit_solution(7008680737794645352)
XLA Ops:
  7.2 0.0 reduce-scatter.13.cloned.1.call-start
  7.2 0.9 fusion.20
  8.1 26.5 %all_gather.12 = bf16[4,8192]{1,0:T(4,128)(2,1)S(1)} all-gather(bf16[4,512]{1,0:T(4,128)(2,1)S(1)} %get-tuple-element.13), channel_id=1, replica_groups=mesh['row'=8,'col'=16] {'col'}, dimensions={1}, use_global_device_ids=true | all-gather | bytes 69632 | tf_op jit(solution)/shard_map/all_gather | solution.py:22
  34.6 0.8 copy.17
  35.4 0.1 reshape.77
  35.5 4.6 fusion.21
  40.0 0.1 broadcast.38.clone
  40.2 2.8 scatter_fusion
  43.0 16.1 %copy.26 = f32[4,65536]{0,1:T(8,128)} copy(f32[4,65536]{1,0:T(4,128)S(1)} %bitcast.65) | data formatting | bytes 2097152
  59.1 0.0 copy-start.1
  59.1 0.0 reduce-scatter.13.cloned.1.call-update
  59.1 0.0 reduce-scatter.15.cloned.1.call-start
  59.2 369.9 %psum.49 = f32[4]{0:T(128)S(1)} all-reduce(f32[4]{0:T(128)S(1)} %get-tuple-element.14), channel_id=1, replica_groups=mesh['row'=8,'col'=16] {'row','col'}, use_global_device_ids=true, to_apply=%region_3.0 | all-reduce | flops 4 | bytes 32 | tf_op jit(solution)/shard_map/psum | solution.py:39
  429.1 0.0 copy-done.1
  429.1 0.1 copy.19
  429.2 0.1 reshape.124
  429.3 0.1 copy.18
  429.4 0.0 reduce-scatter.13.cloned.1.call-done
  429.5 2.8 copy.27
  432.3 0.3 multiply_reduce_fusion.1
  432.6 22.8 %all_gather.13 = bf16[4,65536]{1,0:T(4,128)(2,1)S(1)} all-gather(bf16[4,8192]{1,0:T(4,128)(2,1)S(1)} %convert_element_type.13), channel_id=1, replica_groups=mesh['row'=8,'col'=16] {'row'}, dimensions={1}, use_global_device_ids=true | all-gather | bytes 589824 | tf_op jit(solution)/shard_map/all_gather | solution.py:58
  455.4 0.7 gather_fusion
  456.1 0.0 copy-start
  456.1 5.7 fusion.2
  461.8 2.6 copy.28
  464.4 14.0 %psum.50 = f32[4]{0:T(128)S(1)} all-reduce(f32[4]{0:T(128)S(1)} %get-tuple-element.11), channel_id=1, replica_groups=mesh['row'=8,'col'=16] {'row'}, use_global_device_ids=true, to_apply=%region_5.0 | all-reduce | flops 4 | bytes 32 | tf_op jit(solution)/shard_map/psum | solution.py:43
  478.5 0.0 reduce-scatter.15.cloned.1.call-update
  478.5 0.0 reduce-scatter.17.cloned.1.call-start
  478.5 42.6 %psum.51 = f32[4]{0:T(128)S(1)} all-reduce(f32[4]{0:T(128)S(1)} %psum.50), channel_id=1, replica_groups=mesh['row'=8,'col'=16] {'col'}, use_global_device_ids=true, to_apply=%region_6.0 | all-reduce | flops 4 | bytes 32 | tf_op jit(solution)/shard_map/psum | solution.py:43
  521.1 42.8 %reduce-scatter.15.cloned.1.call-done = f32[512,4]{1,0:T(8,128)} async-done(((f32[8192,4]{1,0:T(8,128)}), f32[512,4]{1,0:T(8,128)}) %reduce-scatter.15.cloned.1.call-update) | async-done | bytes 8208
  563.9 1.1 copy.29
  565.0 0.0 copy-done
  565.0 0.2 multiply_reduce_fusion.2
  565.2 23.1 %all_gather.14 = bf16[4,8192]{1,0:T(4,128)(2,1)S(1)} all-gather(bf16[4,512]{1,0:T(4,128)(2,1)S(1)} %convert_element_type.14), channel_id=1, replica_groups=mesh['row'=8,'col'=16] {'col'}, dimensions={1}, use_global_device_ids=true | all-gather | bytes 69632 | tf_op jit(solution)/shard_map/all_gather | solution.py:22
  588.3 4.6 fusion.22
  592.9 0.1 broadcast.38
  593.1 2.8 scatter_fusion.1
  595.9 16.1 %copy.30 = f32[4,65536]{0,1:T(8,128)} copy(f32[4,65536]{1,0:T(4,128)S(1)} %bitcast.64) | data formatting | bytes 2097152
  612.0 0.0 reduce-scatter.17.cloned.1.call-update
  612.0 0.0 reduce-scatter.19.cloned.1.call-start
  612.1 372.1 %psum.52 = f32[4]{0:T(128)S(1)} all-reduce(f32[4]{0:T(128)S(1)} %get-tuple-element.9), channel_id=1, replica_groups=mesh['row'=8,'col'=16] {'row','col'}, use_global_device_ids=true, to_apply=%region_9.11 | all-reduce | flops 4 | bytes 32 | tf_op jit(solution)/shard_map/psum | solution.py:39
  984.1 0.0 reduce-scatter.17.cloned.1.call-done
  984.1 2.8 copy.31
  987.0 0.1 fusion.19
  987.1 23.0 %all_gather.15 = bf16[4,65536]{1,0:T(4,128)(2,1)S(1)} all-gather(bf16[4,8192]{1,0:T(4,128)(2,1)S(1)} %get-tuple-element.7), channel_id=1, replica_groups=mesh['row'=8,'col'=16] {'row'}, dimensions={1}, use_global_device_ids=true | all-gather | bytes 589824 | tf_op jit(solution)/shard_map/all_gather | solution.py:58
  1010.1 0.7 gather_fusion.1
  1010.8 5.7 fusion
  1016.5 0.2 multiply_reduce_fusion
  1016.7 2.6 copy.32
  1019.3 14.0 %psum.53 = f32[4]{0:T(128)S(1)} all-reduce(f32[4]{0:T(128)S(1)} %multiply_reduce_fusion), channel_id=1, replica_groups=mesh['row'=8,'col'=16] {'row'}, use_global_device_ids=true, to_apply=%region_13.15 | all-reduce | flops 4 | bytes 32 | tf_op jit(solution)/shard_map/psum | solution.py:43
  1033.3 0.0 reduce-scatter.19.cloned.1.call-update
  1033.4 42.6 %psum.54 = f32[4]{0:T(128)S(1)} all-reduce(f32[4]{0:T(128)S(1)} %psum.53), channel_id=1, replica_groups=mesh['row'=8,'col'=16] {'col'}, use_global_device_ids=true, to_apply=%region_14.16 | all-reduce | flops 4 | bytes 32 | tf_op jit(solution)/shard_map/psum | solution.py:43
  1075.9 42.9 %reduce-scatter.19.cloned.1.call-done = f32[512,4]{1,0:T(8,128)} async-done(((f32[8192,4]{1,0:T(8,128)}), f32[512,4]{1,0:T(8,128)}) %reduce-scatter.19.cloned.1.call-update) | async-done | bytes 8208
  1118.9 1.1 copy.33
  1119.9 0.2 fusion.11
  1120.1 65.7 %psum.55 = f32[4]{0:T(128)S(1)} all-reduce(f32[4]{0:T(128)S(1)} %fusion.11), channel_id=1, replica_groups=mesh['row'=8,'col'=16] {'row','col'}, use_global_device_ids=true, to_apply=%region_17.19 | all-reduce | flops 4 | bytes 32 | tf_op jit(solution)/shard_map/psum | solution.py:39
  1185.8 0.6 multiply_divide_fusion
  1186.4 0.8 multiply_add_fusion
  (11 shorter events, 0.1 us)
Async XLA Ops:
  7.2 422.3 %reduce-scatter.13.cloned.1.call-start = ((), (), s32[]{:S(2)}) async-start(), calls=%async_computation.4 | async-start | bytes 37748736
  59.1 370.0 %copy-start.1 = (s32[32,2]{0,1:T(2,128)S(1)}, s32[32,2]{0,1:T(2,128)}, u32[]{:S(2)}) copy-start(s32[32,2]{0,1:T(2,128)} %param.7) | copy-start | bytes 772
  59.1 504.8 %reduce-scatter.15.cloned.1.call-start = ((), (), s32[]{:S(2)}) async-start(), calls=%async_computation.5 | async-start | bytes 4456448
  456.1 108.9 %copy-start = (f32[4,512]{1,0:T(4,128)S(1)}, f32[4,512]{1,0:T(4,128)}, u32[]{:S(2)}) copy-start(f32[4,512]{1,0:T(4,128)} %param.5) | copy-start | bytes 24580
  478.5 505.6 %reduce-scatter.17.cloned.1.call-start = ((), (), s32[]{:S(2)}) async-start(), calls=%async_computation.6 | async-start | bytes 37748736
  612.0 506.9 %reduce-scatter.19.cloned.1.call-start = ((), (), s32[]{:S(2)}) async-start(), calls=%async_computation.7 | async-start | bytes 4456448
Sparse Core Ops, SparseCore 0:
  59.3 325.6 reduce-scatter.12
  478.6 85.2 reduce-scatter.14
  612.1 327.8 reduce-scatter.16
  1033.5 85.3 reduce-scatter.18
